TPU v7x, 32 devices: a whole 2x2x4 slice. The times are simulated.
32 devices in a mesh: patch: 8 (over z, y), rep: 4 (over x, core).
Axes of the slice: x: 2, y: 2, z: 4, core: 2. Of those that a mesh axis runs over, the one named last changes fastest.
Arguments:
- nodes: bfloat16 [4, 4096, 256], P('rep', 'patch'), may hold values from -6 to 6
- edges: bfloat16 [4, 12288, 256], P('rep', 'patch'), may hold values from -6 to 6
- edge_ends: int32 [12288, 2], P('patch'), may hold values from 0 to 543, as said below
- edge_count: int32 [8], P('patch'), may hold values from 768 to 1536, as said below
- send_rows: int32 [16, 16], P('patch'), may hold values from 0 to 511, as said below
- cotangent: bfloat16 [4, 4096, 256], P('rep', 'patch'), may hold values from -6 to 6
- edge_first: bfloat16 [768, 256], replicated, may hold values from -0.21875 to 0.21875
- edge_second: bfloat16 [256, 256], replicated, may hold values from -0.375 to 0.375
- node_first: bfloat16 [512, 256], replicated, may hold values from -0.25 to 0.25
- node_second: bfloat16 [256, 256], replicated, may hold values from -0.375 to 0.375
Outputs:
- new_nodes: bfloat16 [4, 4096, 256], P('rep', 'patch')
- grad_nodes: bfloat16 [4, 4096, 256], P('rep', 'patch')
- grad_edges: bfloat16 [4, 12288, 256], P('rep', 'patch')
- grad_edge_first: bfloat16 [768, 256], replicated
- grad_edge_second: bfloat16 [256, 256], replicated
- grad_node_first: bfloat16 [512, 256], replicated
- grad_node_second: bfloat16 [256, 256], replicated
Inputs may be any that keep to these rules, and one draw needn't show every extreme that they name: `edge_ends`: in patch p's block, row j gives edge slot j: column 0 is a vertex of p; column 1 is a vertex of p, or 512 + h * 16 + s with h < 2, which names the vertex in slot s of row h of the send_rows block of patch (p + h + 1) mod 8. Padding slots hold ends of the same form. `edge_count`: live edge slots of each patch; slots at or beyond it are padding. Some patch has all 1536 live. `send_rows`: each patch's block has 2 rows of 16 distinct vertices of that patch, in its own numbering.
All inputs are finite; a program needn't handle non-finite values.
Results may differ from a plain program's by a relative error of at most 0.0084.
Values may be sent and summed in bfloat16 or wider, within the bound.
A program may use at most 64 MiB of HBM per device.

v0:
```python
import jax
import jax.numpy as jnp
from jax import lax
from jax.sharding import PartitionSpec as P

EPS = 1e-05


def passed_along(block, axis, distance):
    devices = range(lax.axis_size(axis))
    route = [((i - distance) % len(devices), i) for i in devices]
    return lax.ppermute(block, axis, route)


def normalize(values):
    average = jnp.mean(values, axis=-1, keepdims=True)
    centred = values - average
    inv_scale = lax.rsqrt(jnp.mean(centred * centred, axis=-1, keepdims=True) + EPS)
    return (centred * inv_scale, inv_scale)


def norm_back(upstream, normed, inv_scale):
    return inv_scale * (
        upstream
        - jnp.mean(upstream, axis=-1, keepdims=True)
        - normed * jnp.mean(upstream * normed, axis=-1, keepdims=True)
    )


def silu_slope(pre):
    sigma = jax.nn.sigmoid(pre)
    return sigma * (1.0 + pre * (1.0 - sigma))


def matmul(left, right):
    return jnp.dot(left, right, preferred_element_type=jnp.float32)


def outer_sum(left, right):
    return lax.dot_general(
        left, right, (((0,), (0,)), ((), ())), preferred_element_type=jnp.float32
    )


def fetch_seam(outgoing):
    peer_count = outgoing.shape[0]
    pieces = [
        passed_along(outgoing[offset], "patch", -(offset + 1)) for offset in range(peer_count)
    ]
    return jnp.stack(pieces)


def return_seam(totals):
    peer_count = totals.shape[0]
    pieces = [passed_along(totals[offset], "patch", offset + 1) for offset in range(peer_count)]
    return jnp.stack(pieces)


def gather_ends(local_rows, send_rows, first_end, second_end):
    halo = fetch_seam(local_rows[send_rows])
    table = jnp.concatenate([local_rows, halo.reshape(-1, local_rows.shape[1])], axis=0)
    return (local_rows[first_end], table[second_end])


def scatter_ends(first_terms, second_terms, send_rows, first_end, second_end, verts):
    seam_total = send_rows.shape[0] * send_rows.shape[1]
    totals = jax.ops.segment_sum(first_terms, first_end, verts + seam_total) + jax.ops.segment_sum(
        second_terms, second_end, verts + seam_total
    )
    features = totals.shape[1]
    returned = return_seam(totals[verts:].reshape(send_rows.shape + (features,)))
    return totals[:verts].at[send_rows.reshape(-1)].add(returned.reshape(-1, features))


def local(
    nodes,
    edges,
    edge_ends,
    edge_count,
    send_rows,
    cotangent,
    edge_first,
    edge_second,
    node_first,
    node_second,
):
    node_rows = nodes[0]
    edge_rows = edges[0]
    cot_wide = cotangent[0].astype(jnp.float32)
    verts, features = node_rows.shape
    first_end = edge_ends[:, 0]
    second_end = edge_ends[:, 1]
    alive = (jnp.arange(edge_rows.shape[0], dtype=jnp.int32) < edge_count[0]).astype(jnp.float32)[
        :, None
    ]
    first_rows, second_rows = gather_ends(node_rows, send_rows, first_end, second_end)
    edge_pre = (
        matmul(edge_rows, edge_first[:features])
        + matmul(first_rows, edge_first[features : 2 * features])
        + matmul(second_rows, edge_first[2 * features :])
    )
    edge_hidden = jax.nn.silu(edge_pre).astype(jnp.bfloat16)
    edge_normed, edge_inv = normalize(matmul(edge_hidden, edge_second))
    new_edge = ((edge_rows.astype(jnp.float32) + edge_normed) * alive).astype(jnp.bfloat16)
    new_wide = lax.optimization_barrier(new_edge).astype(jnp.float32)
    aggregate = scatter_ends(new_wide, new_wide, send_rows, first_end, second_end, verts).astype(
        jnp.bfloat16
    )
    node_pre = matmul(node_rows, node_first[:features]) + matmul(aggregate, node_first[features:])
    node_hidden = jax.nn.silu(node_pre).astype(jnp.bfloat16)
    node_normed, node_inv = normalize(matmul(node_hidden, node_second))
    new_nodes = (node_rows.astype(jnp.float32) + node_normed).astype(jnp.bfloat16)
    d_node_out = norm_back(cot_wide, node_normed, node_inv).astype(jnp.bfloat16)
    grad_ns = outer_sum(node_hidden, d_node_out)
    d_node_pre = (matmul(d_node_out, node_second.T) * silu_slope(node_pre)).astype(jnp.bfloat16)
    grad_nf = jnp.concatenate(
        [outer_sum(node_rows, d_node_pre), outer_sum(aggregate, d_node_pre)], axis=0
    )
    d_direct = matmul(d_node_pre, node_first[:features].T)
    d_aggregate = matmul(d_node_pre, node_first[features:].T).astype(jnp.bfloat16)
    d_first_rows, d_second_rows = gather_ends(d_aggregate, send_rows, first_end, second_end)
    d_new_edge = alive * (d_first_rows.astype(jnp.float32) + d_second_rows.astype(jnp.float32))
    d_edge_out = norm_back(d_new_edge, edge_normed, edge_inv).astype(jnp.bfloat16)
    grad_es = outer_sum(edge_hidden, d_edge_out)
    d_edge_pre = (matmul(d_edge_out, edge_second.T) * silu_slope(edge_pre)).astype(jnp.bfloat16)
    grad_ef = jnp.concatenate(
        [
            outer_sum(edge_rows, d_edge_pre),
            outer_sum(first_rows, d_edge_pre),
            outer_sum(second_rows, d_edge_pre),
        ],
        axis=0,
    )
    grad_edges = (d_new_edge + matmul(d_edge_pre, edge_first[:features].T)).astype(jnp.bfloat16)
    d_first_end = matmul(d_edge_pre, edge_first[features : 2 * features].T)
    d_second_end = matmul(d_edge_pre, edge_first[2 * features :].T)
    end_terms = scatter_ends(d_first_end, d_second_end, send_rows, first_end, second_end, verts)
    grad_nodes = (cot_wide + d_direct + end_terms).astype(jnp.bfloat16)
    grad_ef, grad_es, grad_nf, grad_ns = lax.psum(
        (grad_ef, grad_es, grad_nf, grad_ns), ("patch", "rep")
    )
    return (
        new_nodes[None],
        grad_nodes[None],
        grad_edges[None],
        grad_ef.astype(jnp.bfloat16),
        grad_es.astype(jnp.bfloat16),
        grad_nf.astype(jnp.bfloat16),
        grad_ns.astype(jnp.bfloat16),
    )


def solution(mesh):
    placed = (
        P("rep", "patch", None),
        P("rep", "patch", None),
        P("patch", None),
        P("patch"),
        P("patch", None),
        P("rep", "patch", None),
        P(),
        P(),
        P(),
        P(),
    )
    return jax.shard_map(
        local,
        mesh=mesh,
        in_specs=placed,
        out_specs=(
            P("rep", "patch", None),
            P("rep", "patch", None),
            P("rep", "patch", None),
            P(),
            P(),
            P(),
            P(),
        ),
        check_vma=False,
    )
```

profile of v0, /device:TPU:0, one launch (start us, length us, event | category | flops | bytes accessed | tf_op | source)
XLA Modules:
  0.0 197.6 jit_solution(6627906289043872199)
XLA Ops:
  1.5 1.6 gather_fusion.1
  3.1 6.1 %collective-permute-start = (bf16[16,256]{1,0:T(8,128)(2,1)S(1)}, bf16[16,256]{1,0:T(8,128)(2,1)S(1)}, u32[]{:S(2)}, u32[]{:S(2)}) collective-permute-start(bf16[16,256]{1,0:T(8,128)(2,1)S(1)} %get-tuple-element.46), channel_id=1, source_target_pairs={{4,0},{8,4},{12,8},{16,12},{20,16},{24,20},{28,24},{0,28},{5,1},{9... | collective-permute-start | bytes 24584 | tf_op jit(solution)/shard_map/ppermute | solution.py:12
  10.3 1.5 slice_reduce_fusion
  11.7 1.1 copy.61
  13.5 2.1 %fusion.38 = f32[512,256]{1,0:T(8,128)} fusion(bf16[512,256]{1,0:T(8,128)(2,1)} %param.18, bf16[1,512,256]{2,1,0:T(8,128)(2,1)} %param.10), kind=kOutput, calls=%fused_computation.80 | convolution fusion | flops 67108864 | bytes 917504 | tf_op jit(solution)/shard_map/dot_general | solution.py:36
  15.6 5.4 %gather_fusion = bf16[1536,256]{1,0:T(8,128)(2,1)} fusion(bf16[512,256]{1,0:T(8,128)(2,1)S(1)} %bitcast.87, s32[2048]{0:T(1024)S(1)} %get-tuple-element.57), kind=kCustom, calls=%fused_computation | custom fusion | bytes 1579008 | tf_op jit(solution)/shard_map/gather | solution.py:62
  22.1 1.5 convolution_add_fusion.2
  25.0 1.2 copy.54
  26.5 5.4 %gather_fusion.2 = bf16[1536,256]{1,0:T(8,128)(2,1)} fusion(bf16[544,256]{1,0:T(8,128)(2,1)S(1)} %copy.58, s32[2048]{0:T(1024)S(1)} %get-tuple-element.56), kind=kCustom, calls=%fused_computation.2 | custom fusion | bytes 1579008 | tf_op jit(solution)/shard_map/gather | solution.py:62
  31.9 2.8 %multiply_convert_fusion.2 = (bf16[1536,256]{1,0:T(8,128)(2,1)S(1)}, f32[1536,256]{1,0:T(8,128)}) fusion(f32[1536,256]{1,0:T(8,128)S(1)} %copy-done.14, bf16[1536,256]{1,0:T(8,128)(2,1)} %gather_fusion.2, bf16[768,256]{1,0:T(8,128)(2,1)} %param.16), kind=kOutput, calls=%fused_computation.24 | convolution fusion | flops 203685888 | bytes 4849664 | tf_op jit(solution)/shard_map/dot_general | solution.py:36
  36.7 1.4 copy.59
  38.1 9.4 %scatter_custom_fusion.1 = f32[544,256]{1,0:T(8,128)S(1)} fusion(s32[1536]{0:T(1024)} %get-tuple-element.30, f32[1536,256]{1,0:T(8,128)} %copy.59, f32[]{:T(128)} %constant.10.clone.1), kind=kCustom, calls=%fused_computation.60 | custom fusion | flops 393216 | bytes 557568 | tf_op jit(solution)/shard_map/scatter-add | solution.py:67
  47.5 10.1 %scatter_custom_fusion = f32[544,256]{1,0:T(8,128)} fusion(s32[1536]{0:T(1024)} %get-tuple-element.33, f32[1536,256]{1,0:T(8,128)} %copy.59, f32[]{:T(128)} %constant.10.clone.1), kind=kCustom, calls=%fused_computation.62 | custom fusion | flops 393216 | bytes 557568 | tf_op jit(solution)/shard_map/scatter-add | solution.py:67
  57.6 1.2 add.126
  59.4 1.0 collective-permute-start.3
  60.5 4.8 %collective-permute-done.2 = f32[16,256]{1,0:T(8,128)S(1)} collective-permute-done((f32[16,256]{1,0:T(8,128)S(1)}, f32[16,256]{1,0:T(8,128)S(1)}, u32[]{:S(2)}, u32[]{:S(2)}) %collective-permute-start.2) | collective-permute-done | bytes 16416 | tf_op jit(solution)/shard_map/ppermute | solution.py:12
  65.3 1.2 scatter_fusion
  66.5 1.4 multiply_convert_fusion.3
  68.8 0.9 fusion.13
  69.7 1.0 fusion.55
  73.5 2.0 %collective-permute-start.4 = (bf16[16,256]{1,0:T(8,128)(2,1)}, bf16[16,256]{1,0:T(8,128)(2,1)}, u32[]{:S(2)}, u32[]{:S(2)}) collective-permute-start(bf16[16,256]{1,0:T(8,128)(2,1)} %get-tuple-element.44), channel_id=1, source_target_pairs={{4,0},{8,4},{12,8},{16,12},{20,16},{24,20},{28,24},{0,28},{5,1},{9... | collective-permute-start | bytes 24584 | tf_op jit(solution)/shard_map/ppermute | solution.py:12
  75.5 0.8 pad_maximum_fusion.1
  76.4 5.4 %gather_fusion.3 = bf16[1536,256]{1,0:T(8,128)(2,1)} fusion(bf16[512,256]{1,0:T(8,128)(2,1)S(1)} %convolution_convert_fusion, s32[2048]{0:T(1024)S(1)} %copy-done.36), kind=kCustom, calls=%fused_computation.3 | custom fusion | bytes 1579008 | tf_op jit(solution)/shard_map/gather | solution.py:62
  81.7 0.8 copy.71
  82.6 1.4 copy.63
  84.8 5.5 %gather_fusion.5 = bf16[1536,256]{1,0:T(8,128)(2,1)} fusion(bf16[544,256]{1,0:T(8,128)(2,1)S(1)} %pad_maximum_fusion.3, s32[2048]{0:T(1024)} %copy-done.34), kind=kCustom, calls=%fused_computation.5 | custom fusion | bytes 1579008 | tf_op jit(solution)/shard_map/gather | solution.py:62
  90.3 1.4 copy.64
  91.7 1.2 fusion.5
  94.1 1.1 fusion.54
  96.8 1.1 fusion.53
  97.9 1.1 fusion.52
  99.0 1.1 convolution_bitcast_fusion.1
  100.1 1.6 fusion.29
  101.7 1.5 fusion.32
  103.2 9.6 %scatter_custom_fusion.4 = f32[544,256]{1,0:T(8,128)S(1)} fusion(s32[1536]{0:T(1024)} %get-tuple-element.30, f32[1536,256]{1,0:T(8,128)} %fusion.29, f32[]{:T(128)} %constant.10.clone.1), kind=kCustom, calls=%fused_computation.56 | custom fusion | flops 393216 | bytes 557568 | tf_op jit(solution)/shard_map/scatter-add | solution.py:67
  112.8 1.1 copy.66
  114.0 10.1 %scatter_custom_fusion.3 = f32[544,256]{1,0:T(8,128)} fusion(s32[1536]{0:T(1024)} %get-tuple-element.33, f32[1536,256]{1,0:T(8,128)} %fusion.32, f32[]{:T(128)} %constant.10.clone.1), kind=kCustom, calls=%fused_computation.58 | custom fusion | flops 393216 | bytes 557568 | tf_op jit(solution)/shard_map/scatter-add | solution.py:67
  124.0 2.2 %copy.65 = f32[544,256]{0,1:T(8,128)} copy(f32[544,256]{1,0:T(8,128)} %scatter_custom_fusion.3) | data formatting | bytes 1114112 | tf_op jit(solution)/shard_map/scatter-add | solution.py:67
  126.2 1.4 add.137
  127.6 1.1 fusion.3
  128.7 0.8 fusion.46
  130.1 1.6 collective-permute-start.7
  131.7 59.5 %all-reduce.2 = (bf16[768,256]{1,0:T(8,128)(2,1)}, bf16[256,256]{1,0:T(8,128)(2,1)}, bf16[512,256]{1,0:T(8,128)(2,1)}, bf16[256,256]{1,0:T(8,128)(2,1)}) all-reduce(f32[768,256]{1,0:T(8,128)S(1)} %pad_maximum_fusion, f32[256,256]{1,0:T(8,128)} %fusion.54, ...), channel_id=1, replica_groups=mesh['patch'=8,'rep'=4] {'patch','rep'}, use_global_device_ids=true, to_apply=%region_14.15 | all-reduce | flops 458752 | bytes 2752512 | tf_op jit(solution)/shard_map/psum | solution.py:139
  191.2 1.3 fusion.2
  192.5 1.2 copy.72
  193.9 1.0 copy.67
  194.8 1.0 copy.68
  195.8 1.0 scatter_fusion.1
  (145 shorter events, 16.3 us)
Async XLA Ops:
  0.6 34.0 %copy-start = (bf16[256,256]{1,0:T(8,128)(2,1)S(1)}, bf16[256,256]{1,0:T(8,128)(2,1)}, u32[]{:S(2)}) copy-start(bf16[256,256]{1,0:T(8,128)(2,1)} %param.17) | copy-start | bytes 393220
  0.6 14.9 %copy-start.1 = (bf16[1,512,256]{2,1,0:T(8,128)(2,1)S(1)}, bf16[1,512,256]{2,1,0:T(8,128)(2,1)}, u32[]{:S(2)}) copy-start(bf16[1,512,256]{2,1,0:T(8,128)(2,1)} %param.10) | copy-start | bytes 786436
  1.5 14.1 %copy-start.37 = (s32[1024]{0:T(1024)}, s32[1024]{0:T(1024)S(1)}, u32[]{:S(2)}) copy-start(s32[1024]{0:T(1024)S(1)} %pad_clamp_fusion.2) | copy-start | bytes 12292
  3.1 23.1 %collective-permute-start = (bf16[16,256]{1,0:T(8,128)(2,1)S(1)}, bf16[16,256]{1,0:T(8,128)(2,1)S(1)}, u32[]{:S(2)}, u32[]{:S(2)}) collective-permute-start(bf16[16,256]{1,0:T(8,128)(2,1)S(1)} %get-tuple-element.46), channel_id=1, source_target_pairs={{4,0},{8,4},{12,8},{16,12},{20,16},{24,20},{28,24},{0,28},{5,1},{9... | collective-permute-start | bytes 24584 | tf_op jit(solution)/shard_map/ppermute | solution.py:12
  9.2 17.0 %collective-permute-start.1 = (bf16[16,256]{1,0:T(8,128)(2,1)S(1)}, bf16[16,256]{1,0:T(8,128)(2,1)S(1)}, u32[]{:S(2)}, u32[]{:S(2)}) collective-permute-start(bf16[16,256]{1,0:T(8,128)(2,1)S(1)} %get-tuple-element.47), channel_id=1, source_target_pairs={{8,0},{12,4},{16,8},{20,12},{24,16},{28,20},{0,24},{4,28},{9,1},{1... | collective-permute-start | bytes 24584 | tf_op jit(solution)/shard_map/ppermute | solution.py:12
  15.5 5.4 %copy-start.35 = (s32[2048]{0:T(1024)}, s32[2048]{0:T(1024)S(1)}, u32[]{:S(2)}) copy-start(s32[2048]{0:T(1024)S(1)} %get-tuple-element.57) | copy-start | bytes 24580
  15.5 10.9 %copy-start.34 = (s32[2048]{0:T(1024)}, s32[2048]{0:T(1024)S(1)}, u32[]{:S(2)}) copy-start(s32[2048]{0:T(1024)S(1)} %get-tuple-element.56) | copy-start | bytes 24580
  15.6 5.4 %copy-start.6 = (bf16[1,1536,256]{2,1,0:T(8,128)(2,1)S(1)}, bf16[1,1536,256]{2,1,0:T(8,128)(2,1)}, u32[]{:S(2)}) copy-start(bf16[1,1536,256]{2,1,0:T(8,128)(2,1)} %param.11) | copy-start | bytes 2359300
  15.6 5.4 %copy-start.15 = (bf16[768,256]{1,0:T(8,128)(2,1)S(1)}, bf16[768,256]{1,0:T(8,128)(2,1)}, u32[]{:S(2)}) copy-start(bf16[768,256]{1,0:T(8,128)(2,1)} %param.16) | copy-start | bytes 1179652
  21.0 1.1 copy-start.9
  22.1 2.1 %copy-start.41 = (s32[2,16]{1,0:T(2,128)S(1)}, s32[2,16]{1,0:T(2,128)}, u32[]{:S(2)}) copy-start(s32[2,16]{1,0:T(2,128)} %param.14) | copy-start | bytes 388
  25.0 1.5 copy-start.11
  26.5 5.4 %copy-start.14 = (f32[1536,256]{1,0:T(8,128)S(1)}, f32[1536,256]{1,0:T(8,128)}, u32[]{:S(2)}) copy-start(f32[1536,256]{1,0:T(8,128)} %convolution_add_fusion.2) | copy-start | bytes 4718596
  34.7 1.4 copy-start.8
  34.7 1.4 copy-start.26
  35.1 1.3 copy-start.29
  38.1 22.3 %copy-start.42 = (s32[32,1]{0,1:T(1,128)S(1)}, s32[32,1]{0,1:T(1,128)}, u32[]{:S(2)}) copy-start(s32[32,1]{0,1:T(1,128)} %reshape.115) | copy-start | bytes 388
  57.6 8.9 %copy-start.20 = (bf16[512,256]{1,0:T(8,128)(2,1)S(1)}, bf16[512,256]{1,0:T(8,128)(2,1)}, u32[]{:S(2)}) copy-start(bf16[512,256]{1,0:T(8,128)(2,1)} %param.18) | copy-start | bytes 786436
  58.8 6.5 %collective-permute-start.2 = (f32[16,256]{1,0:T(8,128)S(1)}, f32[16,256]{1,0:T(8,128)S(1)}, u32[]{:S(2)}, u32[]{:S(2)}) collective-permute-start(f32[16,256]{1,0:T(8,128)S(1)} %get-tuple-element.40), channel_id=1, source_target_pairs={{28,0},{0,4},{4,8},{8,12},{12,16},{16,20},{20,24},{24,28},{29,1},{... | collective-permute-start | bytes 49160 | tf_op jit(solution)/shard_map/ppermute | solution.py:12
  59.4 5.8 %collective-permute-start.3 = (f32[16,256]{1,0:T(8,128)S(1)}, f32[16,256]{1,0:T(8,128)S(1)}, u32[]{:S(2)}, u32[]{:S(2)}) collective-permute-start(f32[16,256]{1,0:T(8,128)S(1)} %get-tuple-element.41), channel_id=1, source_target_pairs={{24,0},{28,4},{0,8},{4,12},{8,16},{12,20},{16,24},{20,28},{25,1},{... | collective-permute-start | bytes 49160 | tf_op jit(solution)/shard_map/ppermute | solution.py:12
  60.5 6.0 %copy-start.39 = (s32[32]{0:T(128)}, s32[32]{0:T(128)S(1)}, u32[]{:S(2)}) copy-start(s32[32]{0:T(128)S(1)} %fusion.43) | copy-start | bytes 388
  66.4 1.4 copy-start.33
  67.8 1.0 copy-start.12
  71.0 5.4 %copy-start.2 = (bf16[512,256]{1,0:T(8,128)(2,1)}, bf16[512,256]{1,0:T(8,128)(2,1)S(1)}, u32[]{:S(2)}) copy-start(bf16[512,256]{1,0:T(8,128)(2,1)S(1)} %fusion.4) | copy-start | bytes 786436
  71.6 4.7 %copy-start.36 = (s32[2048]{0:T(1024)S(1)}, s32[2048]{0:T(1024)}, u32[]{:S(2)}) copy-start(s32[2048]{0:T(1024)} %copy-done.35) | copy-start | bytes 24580
  73.5 10.5 %collective-permute-start.4 = (bf16[16,256]{1,0:T(8,128)(2,1)}, bf16[16,256]{1,0:T(8,128)(2,1)}, u32[]{:S(2)}, u32[]{:S(2)}) collective-permute-start(bf16[16,256]{1,0:T(8,128)(2,1)} %get-tuple-element.44), channel_id=1, source_target_pairs={{4,0},{8,4},{12,8},{16,12},{20,16},{24,20},{28,24},{0,28},{5,1},{9... | collective-permute-start | bytes 24584 | tf_op jit(solution)/shard_map/ppermute | solution.py:12
  75.5 8.5 %collective-permute-start.5 = (bf16[16,256]{1,0:T(8,128)(2,1)S(1)}, bf16[16,256]{1,0:T(8,128)(2,1)}, u32[]{:S(2)}, u32[]{:S(2)}) collective-permute-start(bf16[16,256]{1,0:T(8,128)(2,1)S(1)} %get-tuple-element.45), channel_id=1, source_target_pairs={{8,0},{12,4},{16,8},{20,12},{24,16},{28,20},{0,24},{4,28},{9,1},{1... | collective-permute-start | bytes 24584 | tf_op jit(solution)/shard_map/ppermute | solution.py:12
  76.4 5.4 %copy-start.18 = (bf16[1,512,256]{1,2,0:T(8,128)(2,1)S(1)}, bf16[1,512,256]{1,2,0:T(8,128)(2,1)}, u32[]{:S(2)}) copy-start(bf16[1,512,256]{1,2,0:T(8,128)(2,1)} %get-tuple-element.43) | copy-start | bytes 786436
  90.3 1.4 copy-start.27
  90.3 1.5 copy-start.30
  91.7 1.3 copy-start.32
  93.0 1.1 copy-start.5
  94.1 1.5 copy-start.43
  95.6 1.1 copy-start.19
  96.8 1.1 copy-start.10
  96.8 2.2 %copy-start.7 = (bf16[1,1536,256]{2,1,0:T(8,128)(2,1)S(1)}, bf16[1,1536,256]{2,1,0:T(8,128)(2,1)}, u32[]{:S(2)}) copy-start(bf16[1,1536,256]{2,1,0:T(8,128)(2,1)} %param.11) | copy-start | bytes 2359300
  97.9 2.2 %copy-start.16 = (bf16[768,256]{1,0:T(8,128)(2,1)S(1)}, bf16[768,256]{1,0:T(8,128)(2,1)}, u32[]{:S(2)}) copy-start(bf16[768,256]{1,0:T(8,128)(2,1)} %param.16) | copy-start | bytes 1179652
  124.0 3.5 %copy-start.3 = (bf16[512,256]{1,0:T(8,128)(2,1)S(1)}, bf16[512,256]{1,0:T(8,128)(2,1)}, u32[]{:S(2)}) copy-start(bf16[512,256]{1,0:T(8,128)(2,1)} %copy-done.2) | copy-start | bytes 786436
  124.0 3.6 %copy-start.22 = (bf16[512,256]{1,0:T(8,128)(2,1)S(1)}, bf16[512,256]{1,0:T(8,128)(2,1)}, u32[]{:S(2)}) copy-start(bf16[512,256]{1,0:T(8,128)(2,1)} %param.18) | copy-start | bytes 786436
  127.6 1.9 copy-start.23
  127.6 1.9 copy-start.24
  127.6 1.8 copy-start.25
  128.7 3.0 %copy-start.17 = (f32[256,256]{1,0:T(8,128)S(1)}, f32[256,256]{1,0:T(8,128)}, u32[]{:S(2)}) copy-start(f32[256,256]{1,0:T(8,128)} %fusion.55) | copy-start | bytes 786436
  129.4 61.7 %copy-start.28 = (f32[1536]{0:T(1024)S(1)}, f32[1536]{0:T(1024)}, u32[]{:S(2)}) copy-start(f32[1536]{0:T(1024)} %fusion.40) | copy-start | bytes 18436
  129.5 64.4 %collective-permute-start.6 = (f32[16,256]{0,1:T(8,128)}, f32[16,256]{0,1:T(8,128)}, u32[]{:S(2)}, u32[]{:S(2)}) collective-permute-start(f32[16,256]{0,1:T(8,128)} %get-tuple-element.38), channel_id=1, source_target_pairs={{28,0},{0,4},{4,8},{8,12},{12,16},{16,20},{20,24},{24,28},{29,1},{... | collective-permute-start | bytes 49160 | tf_op jit(solution)/shard_map/ppermute | solution.py:12
  130.1 64.7 %collective-permute-start.7 = (f32[16,256]{0,1:T(8,128)}, f32[16,256]{0,1:T(8,128)}, u32[]{:S(2)}, u32[]{:S(2)}) collective-permute-start(f32[16,256]{0,1:T(8,128)} %get-tuple-element.39), channel_id=1, source_target_pairs={{24,0},{28,4},{0,8},{4,12},{8,16},{12,20},{16,24},{20,28},{25,1},{... | collective-permute-start | bytes 49160 | tf_op jit(solution)/shard_map/ppermute | solution.py:12
  192.5 1.2 copy-start.13
  192.5 3.3 %copy-start.40 = (s32[32]{0:T(128)S(1)}, s32[32]{0:T(128)}, u32[]{:S(2)}) copy-start(s32[32]{0:T(128)} %copy-done.39) | copy-start | bytes 388
  (4 other events, 3.4 us)
where the time goes:
time: 199 us; the launch traced here: 198 us
  blocking collectives  59.5 us (30%)
  other arithmetic  53 us (27%)
  local copies, waits for them, and re-layouts  44.4 us (22%)
  matrix products  21.6 us (11%)
  starting transfers between devices  12.4 us (6%)
  waiting for transfers between devices  4.77 us (2%)
    psum x1, blocking collectives, local(): lax.psum((grad_ef, grad_es, grad_nf, grad_ns), ('patch', 'rep'))  59.5 us
    gather x6, local copies, waits for them, and re-layouts, gather_ends(): return (local_rows[first_end], table[second_end])  24.4 us
    scatter-add x2, other arithmetic, scatter_ends(): jax.ops.segment_sum(first_terms, first_end, verts + seam_total)  20.1 us
    scatter-add x2, other arithmetic, scatter_ends(): jax.ops.segment_sum(second_terms, second_end, verts + seam_total)  19 us
    dot_general x14, matrix products, matmul(): return jnp.dot(left, right, preferred_element_type=jnp.float32)  15.6 us
    ppermute x8, starting transfers between devices, passed_along(): return lax.ppermute(block, axis, route)  12.4 us
    unnamed x93, local copies, waits for them, and re-layouts  8.47 us
    dot_general x7, matrix products, outer_sum(): lax.dot_general(left, right, (((0,), (0,)), ((), ())), preferred_element_...  5.96 us
  transfers between devices with their start and end apart: 8, of which 1 were waited for; matrix products, arithmetic and copies ran while one was open for 14% of the time, Pallas kernels for 0%

commit v1 on v0

v1 whole, which is shorter than its diff:
```python
import functools

import jax
import jax.numpy as jnp
from jax import lax
from jax.experimental import pallas as pl
from jax.experimental.pallas import tpu as pltpu
from jax.sharding import PartitionSpec as P

EPS = 1e-05
MESH = pl.DeviceIdType.MESH
F32 = jnp.float32
BF16 = jnp.bfloat16
LANES = 128
PACK = 16


def mm(left, right):
    return jnp.dot(left, right, preferred_element_type=F32)


def mm_nt(left, right):
    return lax.dot_general(left, right, (((1,), (1,)), ((), ())), preferred_element_type=F32)


def mm_tn(left, right):
    return lax.dot_general(left, right, (((0,), (0,)), ((), ())), preferred_element_type=F32)


def normalize(values):
    average = jnp.mean(values, axis=-1, keepdims=True)
    centred = values - average
    inv_scale = lax.rsqrt(jnp.mean(centred * centred, axis=-1, keepdims=True) + EPS)
    return centred * inv_scale, inv_scale


def norm_back(upstream, normed, inv_scale):
    return inv_scale * (
        upstream
        - jnp.mean(upstream, axis=-1, keepdims=True)
        - normed * jnp.mean(upstream * normed, axis=-1, keepdims=True)
    )


def ones_where(mask):
    return jnp.where(mask, 1.0, 0.0).astype(F32)


def as_column(row):
    n = row.shape[1]
    eye = lax.broadcasted_iota(jnp.int32, (n, n), 0) == lax.broadcasted_iota(jnp.int32, (n, n), 1)
    wide = jnp.broadcast_to(row.astype(F32), (n, n))
    return jnp.sum(jnp.where(eye, wide, 0.0), axis=1, keepdims=True)


def tile_of(total, wanted):
    while total % wanted:
        wanted //= 2
    return wanted


def body(sizes, *refs):
    fused, patches, reps, group = sizes
    (nodes, edges, ends_t, count, send, cot, ef, es, nf, ns) = refs[:10]
    new_nodes, g_nodes, g_edges = refs[10:13]
    rest = refs[13:]
    if fused:
        g_ef, g_es, g_nf, g_ns, acc = rest[:5]
        rest = rest[5:]
    else:
        acc = rest[0]
        rest = rest[1:]
    (cols, pick, tab1, tab2, slope, normed, inv, hidden, msg, halo_src, halo_dst,
     wide, node_pre, node_hidden, d_node_out, d_node_pre, d_tab, sums1, sums2,
     seam_send, seam_recv) = rest[:21]
    rest = rest[21:]
    if fused:
        pair_out, pair_in, chip_sum, ring_in, final, final_other, ar_send, ar_recv = rest

    verts, width = nodes.shape
    slots = edges.shape[0]
    hops, slot = send.shape
    seam = hops * slot
    table = tab2.shape[0]
    tile = tile_of(slots, 256)
    vtile = tile_of(verts, 256)
    me_p = lax.axis_index("patch")
    me_r = lax.axis_index("rep")

    barrier = pltpu.get_barrier_semaphore()
    if fused:
        chips_r = reps // 2
        core = lax.rem(me_r, 2)
        partner = me_r + 1 - 2 * core
        me_g = me_p * chips_r + me_r // 2

        def group_device(k):
            peer = lax.rem(me_g + k, group)
            return peer, {"patch": peer // chips_r, "rep": lax.rem(peer, chips_r) * 2 + core}

        @pl.loop(1, group)
        def _(k):
            _, dev = group_device(k)
            pl.semaphore_signal(barrier, inc=1, device_id=dev, device_id_type=MESH)

        pl.semaphore_signal(barrier, inc=1, device_id={"rep": partner}, device_id_type=MESH)
        greeted = group
    else:
        for step in range(1, hops + 1):
            for other in (lax.rem(me_p + step, patches), lax.rem(me_p + patches - step, patches)):
                pl.semaphore_signal(
                    barrier, inc=1, device_id={"patch": other}, device_id_type=MESH
                )
        greeted = 2 * hops

    def seam_copies(stage):
        down = stage % 2 == 0
        made = []
        for h in range(hops):
            step = patches - h - 1 if down else h + 1
            made.append(
                pltpu.make_async_remote_copy(
                    src_ref=halo_src.at[stage, h],
                    dst_ref=halo_dst.at[stage, h],
                    send_sem=seam_send.at[stage, h],
                    recv_sem=seam_recv.at[stage, h],
                    device_id={"patch": lax.rem(me_p + step, patches)},
                    device_id_type=MESH,
                )
            )
        return made

    def seam_start(stage, values):
        for h in range(hops):
            halo_src[stage, h] = values[h * slot : (h + 1) * slot].astype(BF16)
        for copy in seam_copies(stage):
            copy.start()

    def seam_wait(stage):
        for copy in seam_copies(stage):
            copy.wait()
        return jnp.concatenate([halo_dst[stage, h] for h in range(hops)], axis=0)

    class Bucket:
        def __init__(self, index, row, rows):
            self.index, self.row, self.rows = index, row, rows
            self.first = row // PACK
            self.blocks = rows // PACK
            if fused:
                self.own = self.blocks // group

        def pair(self, phase, src, dst):
            span = pl.ds(self.first, self.blocks)
            return pltpu.make_async_remote_copy(
                src_ref=src.at[span],
                dst_ref=dst.at[span],
                send_sem=ar_send.at[self.index, phase, 0],
                recv_sem=ar_recv.at[self.index, phase, 0],
                device_id={"rep": partner},
                device_id_type=MESH,
            )

        def scatter_copy(self, k):
            peer, dev = group_device(k)
            return pltpu.make_async_remote_copy(
                src_ref=chip_sum.at[pl.ds(self.first + peer * self.own, self.own)],
                dst_ref=ring_in.at[pl.ds(self.first + k * self.own, self.own)],
                send_sem=ar_send.at[self.index, 1, k],
                recv_sem=ar_recv.at[self.index, 1, k],
                device_id=dev,
                device_id_type=MESH,
            )

        def gather_copy(self, k):
            _, dev = group_device(k)
            mine = pl.ds(self.first + me_g * self.own, self.own)
            return pltpu.make_async_remote_copy(
                src_ref=final.at[mine],
                dst_ref=final.at[mine],
                send_sem=ar_send.at[self.index, 2, k],
                recv_sem=ar_recv.at[self.index, 2, k],
                device_id=dev,
                device_id_type=MESH,
            )

        def halves(self):
            low = acc[self.row : self.row + self.rows, :LANES]
            high = acc[self.row : self.row + self.rows, LANES:]
            return low, high

        def start_pair(self):
            if not fused:
                return
            low, high = self.halves()
            other = jnp.where(core == 0, high, low)
            pair_out[self.first : self.first + self.blocks] = other.astype(BF16).reshape(
                self.blocks, PACK, LANES
            )
            self.pair(0, pair_out, pair_in).start()

        def start_scatter(self):
            if not fused:
                return
            self.pair(0, pair_out, pair_in).wait()
            low, high = self.halves()
            mine = jnp.where(core == 0, low, high).reshape(self.blocks, PACK, LANES)
            got = pair_in[self.first : self.first + self.blocks].astype(F32)
            chip_sum[self.first : self.first + self.blocks] = (mine + got).astype(BF16)

            @pl.loop(1, group)
            def _(k):
                self.scatter_copy(k).start()

        def start_gather(self):
            if not fused:
                return

            @pl.loop(1, group)
            def _(k):
                self.scatter_copy(k).wait()

            mine = pl.ds(self.first + me_g * self.own, self.own)
            total = chip_sum[mine].astype(F32)
            for k in range(1, group):
                at = self.first + k * self.own
                total = total + ring_in[at : at + self.own].astype(F32)
            final[mine] = total.astype(BF16)

            @pl.loop(1, group)
            def _(k):
                self.gather_copy(k).start()

        def start_share(self):
            if not fused:
                return

            @pl.loop(1, group)
            def _(k):
                self.gather_copy(k).wait()

            self.pair(3, final, final_other).start()

        def finish(self, targets):
            if not fused:
                return
            self.pair(3, final, final_other).wait()
            at = self.first
            for ref, row, rows in targets:
                n = rows // PACK
                a = final[at : at + n].reshape(rows, LANES)
                b = final_other[at : at + n].reshape(rows, LANES)
                ref[row : row + rows, :LANES] = jnp.where(core == 0, a, b)
                ref[row : row + rows, LANES:] = jnp.where(core == 0, b, a)
                at += n

    node_bucket = Bucket(0, 0, 3 * width)
    mid_bucket = Bucket(1, 3 * width, 2 * width)
    end_bucket = Bucket(2, 5 * width, 2 * width)

    lane_v = lax.broadcasted_iota(jnp.int32, (slot, verts), 1).astype(F32)
    for h in range(hops):
        chosen = as_column(send[h : h + 1, :])
        pick[h * slot : (h + 1) * slot, :] = ones_where(lane_v == chosen).astype(BF16)
    outgoing = mm(pick[...], nodes[...])
    pl.semaphore_wait(barrier, greeted)
    seam_start(0, outgoing)

    @pl.loop(0, slots // LANES)
    def _(j):
        at = pl.ds(pl.multiple_of(j * LANES, LANES), LANES)
        for end in range(2):
            column = as_column(ends_t[end : end + 1, at])
            cols[end, at, :] = jnp.broadcast_to(column, (LANES, LANES)).astype(jnp.int32)

    tab1[...] = mm(nodes[...], ef[width : 2 * width, :]).astype(BF16)
    tab2[0:verts, :] = mm(nodes[...], ef[2 * width :, :]).astype(BF16)
    if table > verts + seam:
        tab2[verts + seam :, :] = jnp.zeros((table - verts - seam, width), BF16)
        d_tab[verts + seam :, :] = jnp.zeros((table - verts - seam, width), BF16)
    halo = seam_wait(0)
    tab2[verts : verts + seam, :] = mm(halo, ef[2 * width :, :]).astype(BF16)

    lane_e = lax.broadcasted_iota(jnp.int32, (tile, LANES), 1)

    def ends_hot(column, size):
        return jnp.concatenate(
            [ones_where(column == lane_e + k) for k in range(0, size, LANES)], axis=1
        )

    def alive_of(start):
        at = lax.broadcasted_iota(jnp.int32, (tile, 1), 0) + start
        return ones_where(at < count[0])

    @pl.loop(0, slots // tile)
    def _(i):
        start = pl.multiple_of(i * tile, tile)
        at = pl.ds(start, tile)
        first = ends_hot(cols[0, at, :], verts).astype(BF16)
        second = ends_hot(cols[1, at, :], table).astype(BF16)
        rows = edges[at, :]
        pre = mm(rows, ef[:width, :]) + mm(first, tab1[...]) + mm(second, tab2[...])
        sigma = jax.nn.sigmoid(pre)
        hid = (pre * sigma).astype(BF16)
        slope[at, :] = sigma * (1.0 + pre * (1.0 - sigma))
        hidden[at, :] = hid
        out, scale = normalize(mm(hid, es[...]))
        normed[at, :] = out
        inv[at, :] = scale
        msg[at, :] = (alive_of(start) * (rows.astype(F32) + out)).astype(BF16)

    sub_v = lax.broadcasted_iota(jnp.int32, (LANES, slots), 0)

    def hot_rows(end, start):
        return ones_where(ends_t[end : end + 1, :] == sub_v + start)

    seam_hot = hot_rows(1, verts).astype(BF16)
    seam_start(1, mm(seam_hot, msg[...])[:seam])

    @pl.loop(0, verts // LANES)
    def _(i):
        start = pl.multiple_of(i * LANES, LANES)
        both = (hot_rows(0, start) + hot_rows(1, start)).astype(BF16)
        wide[pl.ds(start, LANES), :] = mm(both, msg[...])

    node_pre[...] = mm(nodes[...], nf[:width, :])
    returned = seam_wait(1)
    wide[...] += mm_tn(pick[...], returned)
    aggregate = tab1
    aggregate[...] = wide[...].astype(BF16)

    @pl.loop(0, verts // vtile)
    def _(i):
        at = pl.ds(pl.multiple_of(i * vtile, vtile), vtile)
        pre = node_pre[at, :] + mm(aggregate[at, :], nf[width:, :])
        sigma = jax.nn.sigmoid(pre)
        hid = (pre * sigma).astype(BF16)
        node_hidden[at, :] = hid
        out, scale = normalize(mm(hid, ns[...]))
        new_nodes[at, :] = (nodes[at, :].astype(F32) + out).astype(BF16)
        d_out = norm_back(cot[at, :].astype(F32), out, scale).astype(BF16)
        d_node_out[at, :] = d_out
        d_pre = (mm_nt(d_out, ns[...]) * (sigma * (1.0 + pre * (1.0 - sigma)))).astype(BF16)
        d_node_pre[at, :] = d_pre
        d_tab[at, :] = mm_nt(d_pre, nf[width:, :]).astype(BF16)

    seam_start(2, mm(pick[...], d_tab[0:verts, :]))
    acc[0:width, :] = mm_tn(node_hidden[...], d_node_out[...])
    acc[width : 2 * width, :] = mm_tn(nodes[...], d_node_pre[...])
    acc[2 * width : 3 * width, :] = mm_tn(aggregate[...], d_node_pre[...])
    node_bucket.start_pair()
    wide[...] = cot[...].astype(F32) + mm_nt(d_node_pre[...], nf[:width, :])
    acc[3 * width : 5 * width, :] = jnp.zeros((2 * width, width), F32)
    d_tab[verts : verts + seam, :] = seam_wait(2)
    node_bucket.start_scatter()

    d_edge_pre = msg

    @pl.loop(0, slots // tile)
    def _(i):
        start = pl.multiple_of(i * tile, tile)
        at = pl.ds(start, tile)
        both = (
            jnp.concatenate(
                [ends_hot(cols[0, at, :], verts), jnp.zeros((tile, table - verts), F32)], axis=1
            )
            + ends_hot(cols[1, at, :], table)
        ).astype(BF16)
        d_new = alive_of(start) * mm(both, d_tab[...])
        d_out = norm_back(d_new, normed[at, :], inv[at, :]).astype(BF16)
        d_pre = (mm_nt(d_out, es[...]) * slope[at, :]).astype(BF16)
        d_edge_pre[at, :] = d_pre
        g_edges[at, :] = (d_new + mm_nt(d_pre, ef[:width, :])).astype(BF16)
        acc[3 * width : 4 * width, :] += mm_tn(hidden[at, :], d_out)
        acc[4 * width : 5 * width, :] += mm_tn(edges[at, :], d_pre)

    mid_bucket.start_pair()
    seam_sums = mm(seam_hot, d_edge_pre[...])[:seam].astype(BF16)
    seam_start(3, seam_sums)
    node_bucket.start_gather()

    @pl.loop(0, verts // LANES)
    def _(i):
        start = pl.multiple_of(i * LANES, LANES)
        at = pl.ds(start, LANES)
        sums1[at, :] = mm(hot_rows(0, start).astype(BF16), d_edge_pre[...]).astype(BF16)
        sums2[at, :] = mm(hot_rows(1, start).astype(BF16), d_edge_pre[...])

    mid_bucket.start_scatter()
    acc[5 * width : 6 * width, :] = mm_tn(nodes[...], sums1[...])
    acc[6 * width : 7 * width, :] = mm_tn(nodes[...], sums2[...].astype(BF16)) + mm_tn(
        halo, seam_sums
    )
    end_bucket.start_pair()
    part = wide[...] + mm_nt(sums1[...], ef[width : 2 * width, :])
    end_bucket.start_scatter()
    returned = seam_wait(3)
    second = (sums2[...] + mm_tn(pick[...], returned)).astype(BF16)
    g_nodes[...] = (part + mm_nt(second, ef[2 * width :, :])).astype(BF16)
    mid_bucket.start_gather()
    node_bucket.start_share()
    end_bucket.start_gather()
    mid_bucket.start_share()
    if fused:
        node_bucket.finish([(g_ns, 0, width), (g_nf, 0, 2 * width)])
    end_bucket.start_share()
    if fused:
        mid_bucket.finish([(g_es, 0, width), (g_ef, 0, width)])
        end_bucket.finish([(g_ef, width, 2 * width)])


def local(sizes, nodes, edges, edge_ends, edge_count, send_rows, cotangent, ef, es, nf, ns):
    fused, patches, reps, group = sizes
    verts, width = nodes.shape[1:]
    slots = edges.shape[1]
    hops, slot = send_rows.shape
    seam = hops * slot
    table = verts + -(-seam // LANES) * LANES
    rows = ef.shape[0] + es.shape[0] + nf.shape[0] + ns.shape[0]
    vmem = pl.BlockSpec(memory_space=pltpu.VMEM)
    smem = pl.BlockSpec(memory_space=pltpu.SMEM)

    def like(shape, kind=BF16):
        return jax.ShapeDtypeStruct(shape, kind)

    outs = [like((verts, width)), like((verts, width)), like((slots, width))]
    if fused:
        outs += [like(ef.shape), like(es.shape), like(nf.shape), like(ns.shape)]
    else:
        outs += [like((rows, width), F32)]
    scratch = [pltpu.VMEM((rows, width), F32)] if fused else []
    scratch += [
        pltpu.VMEM((2, slots, LANES), jnp.int32),
        pltpu.VMEM((seam, verts), BF16),
        pltpu.VMEM((verts, width), BF16),
        pltpu.VMEM((table, width), BF16),
        pltpu.VMEM((slots, width), F32),
        pltpu.VMEM((slots, width), F32),
        pltpu.VMEM((slots, 1), F32),
        pltpu.VMEM((slots, width), BF16),
        pltpu.VMEM((slots, width), BF16),
        pltpu.VMEM((4, hops, slot, width), BF16),
        pltpu.VMEM((4, hops, slot, width), BF16),
        pltpu.VMEM((verts, width), F32),
        pltpu.VMEM((verts, width), F32),
        pltpu.VMEM((verts, width), BF16),
        pltpu.VMEM((verts, width), BF16),
        pltpu.VMEM((verts, width), BF16),
        pltpu.VMEM((table, width), BF16),
        pltpu.VMEM((verts, width), BF16),
        pltpu.VMEM((verts, width), F32),
        pltpu.SemaphoreType.DMA((4, hops)),
        pltpu.SemaphoreType.DMA((4, hops)),
    ]
    if fused:
        scratch += [pltpu.VMEM((rows // PACK, PACK, LANES), BF16)] * 6
        scratch += [pltpu.SemaphoreType.DMA((3, 4, group))] * 2
    got = pl.pallas_call(
        functools.partial(body, sizes),
        out_shape=outs,
        in_specs=[vmem, vmem, vmem, smem, vmem, vmem, vmem, vmem, vmem, vmem],
        out_specs=[vmem] * len(outs),
        scratch_shapes=scratch,
        compiler_params=pltpu.CompilerParams(
            collective_id=0, has_side_effects=True, vmem_limit_bytes=48 * 2**20
        ),
        name="message_layer",
    )(nodes[0], edges[0], edge_ends.T, edge_count, send_rows, cotangent[0], ef, es, nf, ns)
    new_nodes, g_nodes, g_edges = got[:3]
    if fused:
        g_ef, g_es, g_nf, g_ns = got[3:]
    else:
        total = lax.psum(got[3], ("patch", "rep")).astype(BF16)
        g_ns = total[:width]
        g_nf = total[width : 3 * width]
        g_es = total[3 * width : 4 * width]
        g_ef = total[4 * width :]
    return new_nodes[None], g_nodes[None], g_edges[None], g_ef, g_es, g_nf, g_ns


def solution(mesh):
    patches, reps = mesh.shape["patch"], mesh.shape["rep"]
    group = patches * reps // 2
    fused = reps % 2 == 0 and (2 * LANES) % (PACK * group) == 0
    sizes = (fused, patches, reps, group)
    rows = P("rep", "patch", None)
    placed = (rows, rows, P("patch", None), P("patch"), P("patch", None), rows, P(), P(), P(), P())
    return jax.shard_map(
        functools.partial(local, sizes),
        mesh=mesh,
        in_specs=placed,
        out_specs=(rows, rows, rows, P(), P(), P(), P()),
        check_vma=False,
    )
```

time: 199 us -> 67.2 us (0.34)
  blocking collectives: 59.5 us -> 0 us
  other arithmetic: 53 us -> 0 us
  Pallas kernels: 0 us -> 52.3 us
  local copies, waits for them, and re-layouts: 44.4 us -> 13.2 us
  matrix products: 21.6 us -> 0 us
  starting transfers between devices: 12.4 us -> 0 us
  waiting for transfers between devices: 4.77 us -> 0 us
    psum x1 -> x0, blocking collectives: 59.5 us -> none  [local(): lax.psum((grad_ef, grad_es, grad_nf, grad_ns), ('patch', 'rep'))]
    pallas_call x0 -> x1, Pallas kernels: none -> 52.3 us  [local(): pl.pallas_call(functools.partial(body, sizes), out_shape=outs, in_specs=[...]
    scatter-add x6 -> x0, other arithmetic: 41.2 us -> none  [the longest x2 20.1 us: scatter_ends(): jax.ops.segment_sum(first_terms, first_end, verts + seam_total)]
    gather x8 -> x0, local copies, waits for them, and re-layouts: 26.7 us -> none  [the longest x6 24.4 us: gather_ends(): return (local_rows[first_end], table[second_end])]
    dot_general x21 -> x0, matrix products: 21.6 us -> none  [the longest x14 15.6 us: matmul(): return jnp.dot(left, right, preferred_element_type=jnp.float32)]
    ppermute x8 -> x0, starting transfers between devices: 12.4 us -> none  [passed_along(): return lax.ppermute(block, axis, route)]
    ppermute x8 -> x0, waiting for transfers between devices: 4.77 us -> none  [passed_along(): return lax.ppermute(block, axis, route)]
    unnamed x93 -> x25, local copies, waits for them, and re-layouts: 8.47 us -> 13.2 us
  transfers between devices with their start and end apart: 8 -> 0, of which waited for: 1 -> 0; matrix products, arithmetic and copies ran while one was open for 14% -> 0% of each run, Pallas kernels for 0% -> 0%
where the time goes in v1:
time: 67.2 us; the launch traced here: 66.8 us
  Pallas kernels  52.3 us (78%)
  local copies, waits for them, and re-layouts  13.2 us (20%)
  between operations  1.31 us (2%)
    pallas_call x1, Pallas kernels, local(): pl.pallas_call(functools.partial(body, sizes), out_shape=outs, in_specs=[...  52.3 us
    unnamed x25, local copies, waits for them, and re-layouts  13.2 us

profile of v1, /device:TPU:0, one launch (start us, length us, event | category | flops | bytes accessed | tf_op | source)
XLA Modules:
  0.0 66.8 jit_solution(3115662319850810784)
XLA Ops:
  1.3 0.0 copy-start.8
  1.3 0.7 %copy-done.8 = s32[2,16]{1,0:T(2,128)S(1)} copy-done((s32[2,16]{1,0:T(2,128)S(1)}, s32[2,16]{1,0:T(2,128)}, u32[]{:S(2)}) %copy-start.8) | copy-done | bytes 152
  2.0 0.0 copy-start
  2.0 1.1 %copy-done = bf16[1,1536,256]{2,1,0:T(8,128)(2,1)S(1)} copy-done((bf16[1,1536,256]{2,1,0:T(8,128)(2,1)S(1)}, bf16[1,1536,256]{2,1,0:T(8,128)(2,1)}, u32[]{:S(2)}) %copy-start) | copy-done | bytes 786456
  3.1 0.0 copy-start.1
  3.1 1.0 %copy-done.1 = bf16[768,256]{1,0:T(8,128)(2,1)S(1)} copy-done((bf16[768,256]{1,0:T(8,128)(2,1)S(1)}, bf16[768,256]{1,0:T(8,128)(2,1)}, u32[]{:S(2)}) %copy-start.1) | copy-done | bytes 393240
  4.1 0.0 copy-start.2
  4.1 0.9 %copy-done.2 = bf16[1,512,256]{2,1,0:T(8,128)(2,1)S(1)} copy-done((bf16[1,512,256]{2,1,0:T(8,128)(2,1)S(1)}, bf16[1,512,256]{2,1,0:T(8,128)(2,1)}, u32[]{:S(2)}) %copy-start.2) | copy-done | bytes 262168
  5.0 0.0 copy-start.3
  5.0 0.9 %copy-done.3 = bf16[1,512,256]{2,1,0:T(8,128)(2,1)S(1)} copy-done((bf16[1,512,256]{2,1,0:T(8,128)(2,1)S(1)}, bf16[1,512,256]{2,1,0:T(8,128)(2,1)}, u32[]{:S(2)}) %copy-start.3) | copy-done | bytes 262168
  6.0 0.0 copy-start.4
  6.0 0.9 %copy-done.4 = bf16[512,256]{1,0:T(8,128)(2,1)S(1)} copy-done((bf16[512,256]{1,0:T(8,128)(2,1)S(1)}, bf16[512,256]{1,0:T(8,128)(2,1)}, u32[]{:S(2)}) %copy-start.4) | copy-done | bytes 262168
  6.9 0.0 copy-start.5
  6.9 0.9 %copy-done.5 = bf16[256,256]{1,0:T(8,128)(2,1)S(1)} copy-done((bf16[256,256]{1,0:T(8,128)(2,1)S(1)}, bf16[256,256]{1,0:T(8,128)(2,1)}, u32[]{:S(2)}) %copy-start.5) | copy-done | bytes 131096
  7.8 0.0 copy-start.6
  7.8 0.9 %copy-done.6 = bf16[256,256]{1,0:T(8,128)(2,1)S(1)} copy-done((bf16[256,256]{1,0:T(8,128)(2,1)S(1)}, bf16[256,256]{1,0:T(8,128)(2,1)}, u32[]{:S(2)}) %copy-start.6) | copy-done | bytes 131096
  8.8 0.0 copy-start.7
  8.8 0.7 %copy-done.7 = s32[1536,2]{0,1:T(2,128)S(1)} copy-done((s32[1536,2]{0,1:T(2,128)S(1)}, s32[1536,2]{0,1:T(2,128)}, u32[]{:S(2)}) %copy-start.7) | copy-done | bytes 12312
  9.5 52.3 %message_layer.1 = (bf16[512,256]{1,0:T(8,128)(2,1)S(1)}, bf16[512,256]{1,0:T(8,128)(2,1)S(1)}, bf16[1536,256]{1,0:T(8,128)(2,1)S(1)}, bf16[768,256]{1,0:T(8,128...) custom-call(bf16[512,256]{1,0:T(8,128)(2,1)S(1)} %bitcast.9, ...), custom_call_target="tpu_custom_call" | custom-call | tf_op jit(solution)/shard_map/message_layer/pallas_call | solution.py:457
  61.8 0.7 %copy.25 = bf16[1,512,256]{2,1,0:T(8,128)(2,1)} copy(bf16[1,512,256]{2,1,0:T(8,128)(2,1)S(1)} %bitcast.12) | data formatting | bytes 524288
  62.5 0.7 %copy.26 = bf16[1,512,256]{2,1,0:T(8,128)(2,1)} copy(bf16[1,512,256]{2,1,0:T(8,128)(2,1)S(1)} %bitcast.11) | data formatting | bytes 524288
  63.2 0.9 %copy.27 = bf16[1,1536,256]{2,1,0:T(8,128)(2,1)} copy(bf16[1,1536,256]{2,1,0:T(8,128)(2,1)S(1)} %bitcast.8) | data formatting | bytes 1572864
  64.1 0.7 %copy.28 = bf16[768,256]{1,0:T(8,128)(2,1)} copy(bf16[768,256]{1,0:T(8,128)(2,1)S(1)} %get-tuple-element.31) | data formatting | bytes 786432
  64.8 0.7 copy.29
  65.5 0.7 %copy.30 = bf16[512,256]{1,0:T(8,128)(2,1)} copy(bf16[512,256]{1,0:T(8,128)(2,1)S(1)} %get-tuple-element.33) | data formatting | bytes 524288
  66.2 0.7 copy.31
Async XLA Ops:
  1.3 0.7 %copy-start.8 = (s32[2,16]{1,0:T(2,128)S(1)}, s32[2,16]{1,0:T(2,128)}, u32[]{:S(2)}) copy-start(s32[2,16]{1,0:T(2,128)} %refs_4_.1) | copy-start | bytes 388
  2.0 1.1 %copy-start = (bf16[1,1536,256]{2,1,0:T(8,128)(2,1)S(1)}, bf16[1,1536,256]{2,1,0:T(8,128)(2,1)}, u32[]{:S(2)}) copy-start(bf16[1,1536,256]{2,1,0:T(8,128)(2,1)} %param.11) | copy-start | bytes 2359300
  3.1 1.0 %copy-start.1 = (bf16[768,256]{1,0:T(8,128)(2,1)S(1)}, bf16[768,256]{1,0:T(8,128)(2,1)}, u32[]{:S(2)}) copy-start(bf16[768,256]{1,0:T(8,128)(2,1)} %refs_6_.1) | copy-start | bytes 1179652
  4.1 0.9 %copy-start.2 = (bf16[1,512,256]{2,1,0:T(8,128)(2,1)S(1)}, bf16[1,512,256]{2,1,0:T(8,128)(2,1)}, u32[]{:S(2)}) copy-start(bf16[1,512,256]{2,1,0:T(8,128)(2,1)} %param.10) | copy-start | bytes 786436
  5.0 0.9 %copy-start.3 = (bf16[1,512,256]{2,1,0:T(8,128)(2,1)S(1)}, bf16[1,512,256]{2,1,0:T(8,128)(2,1)}, u32[]{:S(2)}) copy-start(bf16[1,512,256]{2,1,0:T(8,128)(2,1)} %param.15) | copy-start | bytes 786436
  6.0 0.9 %copy-start.4 = (bf16[512,256]{1,0:T(8,128)(2,1)S(1)}, bf16[512,256]{1,0:T(8,128)(2,1)}, u32[]{:S(2)}) copy-start(bf16[512,256]{1,0:T(8,128)(2,1)} %refs_8_.1) | copy-start | bytes 786436
  6.9 0.9 %copy-start.5 = (bf16[256,256]{1,0:T(8,128)(2,1)S(1)}, bf16[256,256]{1,0:T(8,128)(2,1)}, u32[]{:S(2)}) copy-start(bf16[256,256]{1,0:T(8,128)(2,1)} %refs_7_.1) | copy-start | bytes 393220
  7.8 0.9 %copy-start.6 = (bf16[256,256]{1,0:T(8,128)(2,1)S(1)}, bf16[256,256]{1,0:T(8,128)(2,1)}, u32[]{:S(2)}) copy-start(bf16[256,256]{1,0:T(8,128)(2,1)} %refs_9_.1) | copy-start | bytes 393220
  8.8 0.7 %copy-start.7 = (s32[1536,2]{0,1:T(2,128)S(1)}, s32[1536,2]{0,1:T(2,128)}, u32[]{:S(2)}) copy-start(s32[1536,2]{0,1:T(2,128)} %param.12) | copy-start | bytes 36868

commit v2 on v1

--- a/solution.py
+++ b/solution.py
@@ -61,7 +61,8 @@
 
 def body(sizes, *refs):
     fused, patches, reps, group = sizes
-    (nodes, edges, ends_t, count, send, cot, ef, es, nf, ns) = refs[:10]
+    count = refs[3]
+    held = refs[:3] + refs[4:10]
     new_nodes, g_nodes, g_edges = refs[10:13]
     rest = refs[13:]
     if fused:
@@ -73,7 +74,9 @@
     (cols, pick, tab1, tab2, slope, normed, inv, hidden, msg, halo_src, halo_dst,
      wide, node_pre, node_hidden, d_node_out, d_node_pre, d_tab, sums1, sums2,
      seam_send, seam_recv) = rest[:21]
-    rest = rest[21:]
+    (nodes, edges, ends_t, send, cot, ef, es, nf, ns) = rest[21:30]
+    loads = rest[30]
+    rest = rest[31:]
     if fused:
         pair_out, pair_in, chip_sum, ring_in, final, final_other, ar_send, ar_recv = rest
 
@@ -86,6 +89,15 @@
     vtile = tile_of(verts, 256)
     me_p = lax.axis_index("patch")
     me_r = lax.axis_index("rep")
+
+    loaded = [
+        pltpu.make_async_copy(src, dst, loads.at[i])
+        for i, (src, dst) in enumerate(
+            zip(held, (nodes, edges, ends_t, send, cot, ef, es, nf, ns), strict=True)
+        )
+    ]
+    for i in (3, 0, 2, 5, 1, 6, 7, 8, 4):
+        loaded[i].start()
 
     barrier = pltpu.get_barrier_semaphore()
     if fused:
@@ -257,6 +269,8 @@
     mid_bucket = Bucket(1, 3 * width, 2 * width)
     end_bucket = Bucket(2, 5 * width, 2 * width)
 
+    loaded[3].wait()
+    loaded[0].wait()
     lane_v = lax.broadcasted_iota(jnp.int32, (slot, verts), 1).astype(F32)
     for h in range(hops):
         chosen = as_column(send[h : h + 1, :])
@@ -265,6 +279,7 @@
     pl.semaphore_wait(barrier, greeted)
     seam_start(0, outgoing)
 
+    loaded[2].wait()
     @pl.loop(0, slots // LANES)
     def _(j):
         at = pl.ds(pl.multiple_of(j * LANES, LANES), LANES)
@@ -272,11 +287,14 @@
             column = as_column(ends_t[end : end + 1, at])
             cols[end, at, :] = jnp.broadcast_to(column, (LANES, LANES)).astype(jnp.int32)
 
+    loaded[5].wait()
     tab1[...] = mm(nodes[...], ef[width : 2 * width, :]).astype(BF16)
     tab2[0:verts, :] = mm(nodes[...], ef[2 * width :, :]).astype(BF16)
     if table > verts + seam:
         tab2[verts + seam :, :] = jnp.zeros((table - verts - seam, width), BF16)
         d_tab[verts + seam :, :] = jnp.zeros((table - verts - seam, width), BF16)
+    loaded[1].wait()
+    loaded[6].wait()
     halo = seam_wait(0)
     tab2[verts : verts + seam, :] = mm(halo, ef[2 * width :, :]).astype(BF16)
 
@@ -322,6 +340,8 @@
         both = (hot_rows(0, start) + hot_rows(1, start)).astype(BF16)
         wide[pl.ds(start, LANES), :] = mm(both, msg[...])
 
+    for i in (7, 8, 4):
+        loaded[i].wait()
     node_pre[...] = mm(nodes[...], nf[:width, :])
     returned = seam_wait(1)
     wide[...] += mm_tn(pick[...], returned)
@@ -408,6 +428,18 @@
         end_bucket.finish([(g_ef, width, 2 * width)])
 
 
+def write_out(*refs):
+    sems = refs[-1]
+    half = len(refs) // 2
+    copies = [
+        pltpu.make_async_copy(refs[i], refs[half + i], sems.at[i]) for i in range(half)
+    ]
+    for copy in copies:
+        copy.start()
+    for copy in copies:
+        copy.wait()
+
+
 def local(sizes, nodes, edges, edge_ends, edge_count, send_rows, cotangent, ef, es, nf, ns):
     fused, patches, reps, group = sizes
     verts, width = nodes.shape[1:]
@@ -418,6 +450,7 @@
     rows = ef.shape[0] + es.shape[0] + nf.shape[0] + ns.shape[0]
     vmem = pl.BlockSpec(memory_space=pltpu.VMEM)
     smem = pl.BlockSpec(memory_space=pltpu.SMEM)
+    hbm = pl.BlockSpec(memory_space=pltpu.HBM)
 
     def like(shape, kind=BF16):
         return jax.ShapeDtypeStruct(shape, kind)
@@ -451,20 +484,33 @@
         pltpu.SemaphoreType.DMA((4, hops)),
         pltpu.SemaphoreType.DMA((4, hops)),
     ]
+    held = (nodes[0], edges[0], edge_ends.T, send_rows, cotangent[0], ef, es, nf, ns)
+    held = tuple(pltpu.with_memory_space_constraint(x, pltpu.HBM) for x in held)
+    scratch += [pltpu.VMEM(x.shape, x.dtype) for x in held]
+    scratch += [pltpu.SemaphoreType.DMA((len(held),))]
     if fused:
         scratch += [pltpu.VMEM((rows // PACK, PACK, LANES), BF16)] * 6
         scratch += [pltpu.SemaphoreType.DMA((3, 4, group))] * 2
     got = pl.pallas_call(
         functools.partial(body, sizes),
         out_shape=outs,
-        in_specs=[vmem, vmem, vmem, smem, vmem, vmem, vmem, vmem, vmem, vmem],
+        in_specs=[hbm] * 3 + [smem] + [hbm] * 6,
         out_specs=[vmem] * len(outs),
         scratch_shapes=scratch,
         compiler_params=pltpu.CompilerParams(
             collective_id=0, has_side_effects=True, vmem_limit_bytes=48 * 2**20
         ),
         name="message_layer",
-    )(nodes[0], edges[0], edge_ends.T, edge_count, send_rows, cotangent[0], ef, es, nf, ns)
+    )(*held[:3], edge_count, *held[3:])
+    got = pl.pallas_call(
+        write_out,
+        out_shape=outs,
+        in_specs=[vmem] * len(outs),
+        out_specs=[hbm] * len(outs),
+        scratch_shapes=[pltpu.SemaphoreType.DMA((len(outs),))],
+        compiler_params=pltpu.CompilerParams(vmem_limit_bytes=2**20),
+        name="write_out",
+    )(*got)
     new_nodes, g_nodes, g_edges = got[:3]
     if fused:
         g_ef, g_es, g_nf, g_ns = got[3:]

time: 67.2 us -> 55.4 us (0.82)
  local copies, waits for them, and re-layouts: 13.2 us -> 0 us
  Pallas kernels: 52.3 us -> 53.9 us
    unnamed x25 -> x0, local copies, waits for them, and re-layouts: 13.2 us -> none
    pallas_call x0 -> x1, Pallas kernels: none -> 1.41 us  [local(): pl.pallas_call(write_out, out_shape=outs, in_specs=[vmem] * len(outs), ou...]
where the time goes in v2:
time: 55.4 us; the launch traced here: 55.2 us
  Pallas kernels  53.9 us (97%)
  between operations  1.29 us (2%)
    pallas_call x1, Pallas kernels, local(): pl.pallas_call(functools.partial(body, sizes), out_shape=outs, in_specs=[...  52.5 us
    pallas_call x1, Pallas kernels, local(): pl.pallas_call(write_out, out_shape=outs, in_specs=[vmem] * len(outs), ou...  1.41 us

profile of v2, /device:TPU:0, one launch (start us, length us, event | category | flops | bytes accessed | tf_op | source)
XLA Modules:
  0.0 55.2 jit_solution(6432364414919113261)
XLA Ops:
  1.3 52.5 %message_layer.1 = (bf16[512,256]{1,0:T(8,128)(2,1)S(1)}, bf16[512,256]{1,0:T(8,128)(2,1)S(1)}, bf16[1536,256]{1,0:T(8,128)(2,1)S(1)}, bf16[768,256]{1,0:T(8,128...) custom-call(bf16[512,256]{1,0:T(8,128)(2,1)} %bitcast.8, ...), custom_call_target="tpu_custom_call" | custom-call | tf_op jit(solution)/shard_map/message_layer/pallas_call | solution.py:494
  53.8 1.4 %write_out.1 = (bf16[512,256]{1,0:T(8,128)(2,1)}, bf16[512,256]{1,0:T(8,128)(2,1)}, bf16[1536,256]{1,0:T(8,128)(2,1)}, bf16[768,256]{1,0:T(8,128)(2,1)}, bf16[25...) custom-call(bf16[512,256]{1,0:T(8,128)(2,1)S(1)} %get-tuple-element.21.refs_0_, ...), custom_call_target="tpu_custom_call" | custom-call | tf_op jit(solution)/shard_map/write_out/pallas_call | solution.py:505

commit v3 on v2

--- a/solution.py
+++ b/solution.py
@@ -74,9 +74,10 @@
     (cols, pick, tab1, tab2, slope, normed, inv, hidden, msg, halo_src, halo_dst,
      wide, node_pre, node_hidden, d_node_out, d_node_pre, d_tab, sums1, sums2,
      seam_send, seam_recv) = rest[:21]
-    (nodes, edges, ends_t, send, cot, ef, es, nf, ns) = rest[21:30]
-    loads = rest[30]
-    rest = rest[31:]
+    d_new_edge = rest[21]
+    (nodes, edges, ends_t, send, cot, ef, es, nf, ns) = rest[22:31]
+    loads = rest[31]
+    rest = rest[32:]
     if fused:
         pair_out, pair_in, chip_sum, ring_in, final, final_other, ar_send, ar_recv = rest
 
@@ -143,8 +144,9 @@
         return made
 
     def seam_start(stage, values):
-        for h in range(hops):
-            halo_src[stage, h] = values[h * slot : (h + 1) * slot].astype(BF16)
+        if values is not None:
+            for h in range(hops):
+                halo_src[stage, h] = values[h * slot : (h + 1) * slot].astype(BF16)
         for copy in seam_copies(stage):
             copy.start()
 
@@ -276,8 +278,8 @@
         chosen = as_column(send[h : h + 1, :])
         pick[h * slot : (h + 1) * slot, :] = ones_where(lane_v == chosen).astype(BF16)
     outgoing = mm(pick[...], nodes[...])
-    pl.semaphore_wait(barrier, greeted)
-    seam_start(0, outgoing)
+    for h in range(hops):
+        halo_src[0, h] = outgoing[h * slot : (h + 1) * slot].astype(BF16)
 
     loaded[2].wait()
     @pl.loop(0, slots // LANES)
@@ -293,11 +295,6 @@
     if table > verts + seam:
         tab2[verts + seam :, :] = jnp.zeros((table - verts - seam, width), BF16)
         d_tab[verts + seam :, :] = jnp.zeros((table - verts - seam, width), BF16)
-    loaded[1].wait()
-    loaded[6].wait()
-    halo = seam_wait(0)
-    tab2[verts : verts + seam, :] = mm(halo, ef[2 * width :, :]).astype(BF16)
-
     lane_e = lax.broadcasted_iota(jnp.int32, (tile, LANES), 1)
 
     def ends_hot(column, size):
@@ -309,14 +306,35 @@
         at = lax.broadcasted_iota(jnp.int32, (tile, 1), 0) + start
         return ones_where(at < count[0])
 
-    @pl.loop(0, slots // tile)
+    def halo_hot(at):
+        return jnp.concatenate(
+            [ones_where(cols[1, at, :] == lane_e + k) for k in range(verts, table, LANES)], axis=1
+        ).astype(BF16)
+
+    def local_pre(i):
+        at = pl.ds(pl.multiple_of(i * tile, tile), tile)
+        first = ends_hot(cols[0, at, :], verts).astype(BF16)
+        second = ends_hot(cols[1, at, :], verts).astype(BF16)
+        slope[at, :] = (
+            mm(edges[at, :], ef[:width, :]) + mm(first, tab1[...]) + mm(second, tab2[:verts, :])
+        )
+
+    loaded[1].wait()
+    tiles = slots // tile
+    pl.loop(0, tiles // 3)(local_pre)
+    pl.semaphore_wait(barrier, greeted)
+    seam_start(0, None)
+    pl.loop(tiles // 3, tiles)(local_pre)
+    loaded[6].wait()
+    halo = seam_wait(0)
+    tab2[verts : verts + seam, :] = mm(halo, ef[2 * width :, :]).astype(BF16)
+
+    @pl.loop(0, tiles)
     def _(i):
         start = pl.multiple_of(i * tile, tile)
         at = pl.ds(start, tile)
-        first = ends_hot(cols[0, at, :], verts).astype(BF16)
-        second = ends_hot(cols[1, at, :], table).astype(BF16)
         rows = edges[at, :]
-        pre = mm(rows, ef[:width, :]) + mm(first, tab1[...]) + mm(second, tab2[...])
+        pre = slope[at, :] + mm(halo_hot(at), tab2[verts:, :])
         sigma = jax.nn.sigmoid(pre)
         hid = (pre * sigma).astype(BF16)
         slope[at, :] = sigma * (1.0 + pre * (1.0 - sigma))
@@ -370,26 +388,28 @@
     node_bucket.start_pair()
     wide[...] = cot[...].astype(F32) + mm_nt(d_node_pre[...], nf[:width, :])
     acc[3 * width : 5 * width, :] = jnp.zeros((2 * width, width), F32)
+
+    def local_d_new(i):
+        at = pl.ds(pl.multiple_of(i * tile, tile), tile)
+        both = (ends_hot(cols[0, at, :], verts) + ends_hot(cols[1, at, :], verts)).astype(BF16)
+        d_new_edge[at, :] = mm(both, d_tab[:verts, :])
+
+    pl.loop(0, tiles // 2)(local_d_new)
+    node_bucket.start_scatter()
+    pl.loop(tiles // 2, tiles)(local_d_new)
     d_tab[verts : verts + seam, :] = seam_wait(2)
-    node_bucket.start_scatter()
 
     d_edge_pre = msg
 
-    @pl.loop(0, slots // tile)
+    @pl.loop(0, tiles)
     def _(i):
         start = pl.multiple_of(i * tile, tile)
         at = pl.ds(start, tile)
-        both = (
-            jnp.concatenate(
-                [ends_hot(cols[0, at, :], verts), jnp.zeros((tile, table - verts), F32)], axis=1
-            )
-            + ends_hot(cols[1, at, :], table)
-        ).astype(BF16)
-        d_new = alive_of(start) * mm(both, d_tab[...])
+        d_new = alive_of(start) * (d_new_edge[at, :] + mm(halo_hot(at), d_tab[verts:, :]))
+        d_new_edge[at, :] = d_new
         d_out = norm_back(d_new, normed[at, :], inv[at, :]).astype(BF16)
         d_pre = (mm_nt(d_out, es[...]) * slope[at, :]).astype(BF16)
         d_edge_pre[at, :] = d_pre
-        g_edges[at, :] = (d_new + mm_nt(d_pre, ef[:width, :])).astype(BF16)
         acc[3 * width : 4 * width, :] += mm_tn(hidden[at, :], d_out)
         acc[4 * width : 5 * width, :] += mm_tn(edges[at, :], d_pre)
 
@@ -413,6 +433,12 @@
     end_bucket.start_pair()
     part = wide[...] + mm_nt(sums1[...], ef[width : 2 * width, :])
     end_bucket.start_scatter()
+
+    @pl.loop(0, tiles)
+    def _(i):
+        at = pl.ds(pl.multiple_of(i * tile, tile), tile)
+        g_edges[at, :] = (d_new_edge[at, :] + mm_nt(d_edge_pre[at, :], ef[:width, :])).astype(BF16)
+
     returned = seam_wait(3)
     second = (sums2[...] + mm_tn(pick[...], returned)).astype(BF16)
     g_nodes[...] = (part + mm_nt(second, ef[2 * width :, :])).astype(BF16)
@@ -483,6 +509,7 @@
         pltpu.VMEM((verts, width), F32),
         pltpu.SemaphoreType.DMA((4, hops)),
         pltpu.SemaphoreType.DMA((4, hops)),
+        pltpu.VMEM((slots, width), F32),
     ]
     held = (nodes[0], edges[0], edge_ends.T, send_rows, cotangent[0], ef, es, nf, ns)
     held = tuple(pltpu.with_memory_space_constraint(x, pltpu.HBM) for x in held)

time: 55.4 us -> 53.6 us (0.968)
  Pallas kernels: 53.9 us -> 52.2 us
    pallas_call x1, Pallas kernels: 52.5 us -> 50.8 us  [local(): pl.pallas_call(functools.partial(body, sizes), out_shape=outs, in_specs=[...]
where the time goes in v3:
time: 53.6 us; the launch traced here: 53.5 us
  Pallas kernels  52.2 us (97%)
  between operations  1.29 us (2%)
    pallas_call x1, Pallas kernels, local(): pl.pallas_call(functools.partial(body, sizes), out_shape=outs, in_specs=[...  50.8 us
    pallas_call x1, Pallas kernels, local(): pl.pallas_call(write_out, out_shape=outs, in_specs=[vmem] * len(outs), ou...  1.41 us

profile of v3, /device:TPU:0, one launch (start us, length us, event | category | flops | bytes accessed | tf_op | source)
XLA Modules:
  0.0 53.5 jit_solution(8596766716029072470)
XLA Ops:
  1.3 50.8 %message_layer.1 = (bf16[512,256]{1,0:T(8,128)(2,1)S(1)}, bf16[512,256]{1,0:T(8,128)(2,1)S(1)}, bf16[1536,256]{1,0:T(8,128)(2,1)S(1)}, bf16[768,256]{1,0:T(8,128...) custom-call(bf16[512,256]{1,0:T(8,128)(2,1)} %bitcast.8, ...), custom_call_target="tpu_custom_call" | custom-call | tf_op jit(solution)/shard_map/message_layer/pallas_call | solution.py:521
  52.1 1.4 %write_out.1 = (bf16[512,256]{1,0:T(8,128)(2,1)}, bf16[512,256]{1,0:T(8,128)(2,1)}, bf16[1536,256]{1,0:T(8,128)(2,1)}, bf16[768,256]{1,0:T(8,128)(2,1)}, bf16[25...) custom-call(bf16[512,256]{1,0:T(8,128)(2,1)S(1)} %get-tuple-element.21.refs_0_, ...), custom_call_target="tpu_custom_call" | custom-call | tf_op jit(solution)/shard_map/write_out/pallas_call | solution.py:532

commit v4 on v3

--- a/solution.py
+++ b/solution.py
@@ -13,6 +13,7 @@
 BF16 = jnp.bfloat16
 LANES = 128
 PACK = 16
+INNER = 2
 
 
 def mm(left, right):
@@ -79,7 +80,7 @@
     loads = rest[31]
     rest = rest[32:]
     if fused:
-        pair_out, pair_in, chip_sum, ring_in, final, final_other, ar_send, ar_recv = rest
+        pair_out, pair_in, chip_sum, ring_in, final, final_other, line_sum, ar_send, ar_recv = rest
 
     verts, width = nodes.shape
     slots = edges.shape[0]
@@ -105,26 +106,35 @@
         chips_r = reps // 2
         core = lax.rem(me_r, 2)
         partner = me_r + 1 - 2 * core
-        me_g = me_p * chips_r + me_r // 2
-
-        def group_device(k):
-            peer = lax.rem(me_g + k, group)
-            return peer, {"patch": peer // chips_r, "rep": lax.rem(peer, chips_r) * 2 + core}
-
-        @pl.loop(1, group)
-        def _(k):
-            _, dev = group_device(k)
-            pl.semaphore_signal(barrier, inc=1, device_id=dev, device_id_type=MESH)
-
-        pl.semaphore_signal(barrier, inc=1, device_id={"rep": partner}, device_id_type=MESH)
-        greeted = group
+        quad, lines = INNER * chips_r, patches // INNER
+        me_l, me_y = me_p // INNER, lax.rem(me_p, INNER)
+        me_q = me_y * chips_r + me_r // 2
+
+        def quad_device(k):
+            peer = lax.rem(me_q + k, quad)
+            return peer, {
+                "patch": me_l * INNER + peer // chips_r,
+                "rep": lax.rem(peer, chips_r) * 2 + core,
+            }
+
+        def line_device(k):
+            return {"patch": lax.rem(me_l + k, lines) * INNER + me_y}
+
+        def greet(device):
+            pl.semaphore_signal(barrier, inc=1, device_id=device, device_id_type=MESH)
+
+        for k in range(1, quad):
+            greet(quad_device(k)[1])
+        for k in range(1, lines):
+            greet(line_device(k))
+        greet({"rep": partner})
+        greeted = quad + lines - 1
     else:
-        for step in range(1, hops + 1):
-            for other in (lax.rem(me_p + step, patches), lax.rem(me_p + patches - step, patches)):
-                pl.semaphore_signal(
-                    barrier, inc=1, device_id={"patch": other}, device_id_type=MESH
-                )
-        greeted = 2 * hops
+        greeted = 0
+    for step in range(1, hops + 1):
+        for other in (lax.rem(me_p + step, patches), lax.rem(me_p + patches - step, patches)):
+            pl.semaphore_signal(barrier, inc=1, device_id={"patch": other}, device_id_type=MESH)
+    greeted += 2 * hops
 
     def seam_copies(stage):
         down = stage % 2 == 0
@@ -161,7 +171,8 @@
             self.first = row // PACK
             self.blocks = rows // PACK
             if fused:
-                self.own = self.blocks // group
+                self.own = self.blocks // quad
+                self.line_first = self.first * lines // quad
 
         def pair(self, phase, src, dst):
             span = pl.ds(self.first, self.blocks)
@@ -175,7 +186,7 @@
             )
 
         def scatter_copy(self, k):
-            peer, dev = group_device(k)
+            peer, dev = quad_device(k)
             return pltpu.make_async_remote_copy(
                 src_ref=chip_sum.at[pl.ds(self.first + peer * self.own, self.own)],
                 dst_ref=ring_in.at[pl.ds(self.first + k * self.own, self.own)],
@@ -185,14 +196,25 @@
                 device_id_type=MESH,
             )
 
+        def line_copy(self, k):
+            mine = pl.ds(self.line_first + me_l * self.own, self.own)
+            return pltpu.make_async_remote_copy(
+                src_ref=line_sum.at[mine],
+                dst_ref=line_sum.at[mine],
+                send_sem=ar_send.at[self.index, 2, k],
+                recv_sem=ar_recv.at[self.index, 2, k],
+                device_id=line_device(k),
+                device_id_type=MESH,
+            )
+
         def gather_copy(self, k):
-            _, dev = group_device(k)
-            mine = pl.ds(self.first + me_g * self.own, self.own)
+            _, dev = quad_device(k)
+            mine = pl.ds(self.first + me_q * self.own, self.own)
             return pltpu.make_async_remote_copy(
                 src_ref=final.at[mine],
                 dst_ref=final.at[mine],
-                send_sem=ar_send.at[self.index, 2, k],
-                recv_sem=ar_recv.at[self.index, 2, k],
+                send_sem=ar_send.at[self.index, 3, k],
+                recv_sem=ar_recv.at[self.index, 3, k],
                 device_id=dev,
                 device_id_type=MESH,
             )
@@ -221,43 +243,45 @@
             got = pair_in[self.first : self.first + self.blocks].astype(F32)
             chip_sum[self.first : self.first + self.blocks] = (mine + got).astype(BF16)
 
-            @pl.loop(1, group)
-            def _(k):
+            for k in range(1, quad):
                 self.scatter_copy(k).start()
+
+        def start_line(self):
+            if not fused:
+                return
+            total = chip_sum[pl.ds(self.first + me_q * self.own, self.own)].astype(F32)
+            for k in range(1, quad):
+                self.scatter_copy(k).wait()
+                at = self.first + k * self.own
+                total = total + ring_in[at : at + self.own].astype(F32)
+            line_sum[pl.ds(self.line_first + me_l * self.own, self.own)] = total.astype(BF16)
+            for k in range(1, lines):
+                self.line_copy(k).start()
 
         def start_gather(self):
             if not fused:
                 return
-
-            @pl.loop(1, group)
-            def _(k):
-                self.scatter_copy(k).wait()
-
-            mine = pl.ds(self.first + me_g * self.own, self.own)
-            total = chip_sum[mine].astype(F32)
-            for k in range(1, group):
-                at = self.first + k * self.own
-                total = total + ring_in[at : at + self.own].astype(F32)
-            final[mine] = total.astype(BF16)
-
-            @pl.loop(1, group)
-            def _(k):
+            for k in range(1, lines):
+                self.line_copy(k).wait()
+            total = line_sum[self.line_first : self.line_first + self.own].astype(F32)
+            for k in range(1, lines):
+                at = self.line_first + k * self.own
+                total = total + line_sum[at : at + self.own].astype(F32)
+            final[pl.ds(self.first + me_q * self.own, self.own)] = total.astype(BF16)
+            for k in range(1, quad):
                 self.gather_copy(k).start()
 
         def start_share(self):
             if not fused:
                 return
-
-            @pl.loop(1, group)
-            def _(k):
+            for k in range(1, quad):
                 self.gather_copy(k).wait()
-
-            self.pair(3, final, final_other).start()
+            self.pair(4, final, final_other).start()
 
         def finish(self, targets):
             if not fused:
                 return
-            self.pair(3, final, final_other).wait()
+            self.pair(4, final, final_other).wait()
             at = self.first
             for ref, row, rows in targets:
                 n = rows // PACK
@@ -416,7 +440,7 @@
     mid_bucket.start_pair()
     seam_sums = mm(seam_hot, d_edge_pre[...])[:seam].astype(BF16)
     seam_start(3, seam_sums)
-    node_bucket.start_gather()
+    node_bucket.start_line()
 
     @pl.loop(0, verts // LANES)
     def _(i):
@@ -426,12 +450,14 @@
         sums2[at, :] = mm(hot_rows(1, start).astype(BF16), d_edge_pre[...])
 
     mid_bucket.start_scatter()
+    node_bucket.start_gather()
     acc[5 * width : 6 * width, :] = mm_tn(nodes[...], sums1[...])
     acc[6 * width : 7 * width, :] = mm_tn(nodes[...], sums2[...].astype(BF16)) + mm_tn(
         halo, seam_sums
     )
     end_bucket.start_pair()
     part = wide[...] + mm_nt(sums1[...], ef[width : 2 * width, :])
+    mid_bucket.start_line()
     end_bucket.start_scatter()
 
     @pl.loop(0, tiles)
@@ -439,6 +465,7 @@
         at = pl.ds(pl.multiple_of(i * tile, tile), tile)
         g_edges[at, :] = (d_new_edge[at, :] + mm_nt(d_edge_pre[at, :], ef[:width, :])).astype(BF16)
 
+    end_bucket.start_line()
     returned = seam_wait(3)
     second = (sums2[...] + mm_tn(pick[...], returned)).astype(BF16)
     g_nodes[...] = (part + mm_nt(second, ef[2 * width :, :])).astype(BF16)
@@ -517,7 +544,9 @@
     scratch += [pltpu.SemaphoreType.DMA((len(held),))]
     if fused:
         scratch += [pltpu.VMEM((rows // PACK, PACK, LANES), BF16)] * 6
-        scratch += [pltpu.SemaphoreType.DMA((3, 4, group))] * 2
+        quad, lines = INNER * reps // 2, patches // INNER
+        scratch += [pltpu.VMEM((rows // PACK * lines // quad, PACK, LANES), BF16)]
+        scratch += [pltpu.SemaphoreType.DMA((3, 5, max(quad, lines)))] * 2
     got = pl.pallas_call(
         functools.partial(body, sizes),
         out_shape=outs,
@@ -553,7 +582,7 @@
 def solution(mesh):
     patches, reps = mesh.shape["patch"], mesh.shape["rep"]
     group = patches * reps // 2
-    fused = reps % 2 == 0 and (2 * LANES) % (PACK * group) == 0
+    fused = reps % 2 == 0 and patches % INNER == 0 and (2 * LANES) % (PACK * group) == 0
     sizes = (fused, patches, reps, group)
     rows = P("rep", "patch", None)
     placed = (rows, rows, P("patch", None), P("patch"), P("patch", None), rows, P(), P(), P(), P())

time: 53.6 us -> 51 us (0.951)
  Pallas kernels: 52.2 us -> 49.5 us
    pallas_call x1, Pallas kernels: 50.8 us -> 48.1 us  [local(): pl.pallas_call(functools.partial(body, sizes), out_shape=outs, in_specs=[...]
where the time goes in v4:
time: 51 us; the launch traced here: 50.8 us
  Pallas kernels  49.5 us (97%)
  between operations  1.29 us (3%)
    pallas_call x1, Pallas kernels, local(): pl.pallas_call(functools.partial(body, sizes), out_shape=outs, in_specs=[...  48.1 us
    pallas_call x1, Pallas kernels, local(): pl.pallas_call(write_out, out_shape=outs, in_specs=[vmem] * len(outs), ou...  1.41 us

profile of v4, /device:TPU:0, one launch (start us, length us, event | category | flops | bytes accessed | tf_op | source)
XLA Modules:
  0.0 50.8 jit_solution(11851694536165193766)
XLA Ops:
  1.3 48.1 %message_layer.1 = (bf16[512,256]{1,0:T(8,128)(2,1)S(1)}, bf16[512,256]{1,0:T(8,128)(2,1)S(1)}, bf16[1536,256]{1,0:T(8,128)(2,1)S(1)}, bf16[768,256]{1,0:T(8,128...) custom-call(bf16[512,256]{1,0:T(8,128)(2,1)} %bitcast.8, ...), custom_call_target="tpu_custom_call" | custom-call | tf_op jit(solution)/shard_map/message_layer/pallas_call | solution.py:550
  49.4 1.4 %write_out.1 = (bf16[512,256]{1,0:T(8,128)(2,1)}, bf16[512,256]{1,0:T(8,128)(2,1)}, bf16[1536,256]{1,0:T(8,128)(2,1)}, bf16[768,256]{1,0:T(8,128)(2,1)}, bf16[25...) custom-call(bf16[512,256]{1,0:T(8,128)(2,1)S(1)} %get-tuple-element.21.refs_0_, ...), custom_call_target="tpu_custom_call" | custom-call | tf_op jit(solution)/shard_map/write_out/pallas_call | solution.py:561
